TPU v7x, 512 devices: a whole 4x4x16 slice. The times are simulated.
512 devices in a mesh: src: 32 (over y, x, core), tgt: 16 (over z).
Axes of the slice: x: 4, y: 4, z: 16, core: 2. Of those that a mesh axis runs over, the one named last changes fastest.
Arguments:
- src_cells: float32 [50, 131072], P(None, ('src', 'tgt')), may hold values from -0.8 to 0.8
- tgt_cells: float32 [50, 8192], P(None, 'tgt'), may hold values from -0.8 to 0.8
- src_mass: float32 [131072], P('src'), may hold values from 0.5 to 2
- tgt_mass: float32 [8192], P('tgt'), may hold values from 0.5 to 2
Outputs:
- src_potential: float32 [131072], P('src')
- tgt_potential: float32 [8192], P('tgt')
All inputs are finite; a program needn't handle non-finite values.
Results may differ from a plain program's by a relative error of at most 0.00015.
Values sent between devices are 32-bit elements; how exact they have to be, the bound alone decides.
No kernel may reach another device: no remote copies, remote signals or barrier semaphores. Data moves between devices by JAX's collectives and lax.ppermute only.
A program may use at most 64 MiB of HBM per device.

v0:
```python
import jax
import jax.numpy as jnp
from jax import lax
from jax.sharding import PartitionSpec as P

ITERS = 2
epsilon_reg = 2.0


def gibbs_tile(src_block, tgt_block):
    src_norm = jnp.sum(src_block * src_block, axis=0)
    tgt_norm = jnp.sum(tgt_block * tgt_block, axis=0)
    cross = jnp.dot(
        src_block.T, tgt_block, precision=lax.Precision.HIGHEST, preferred_element_type=jnp.float32
    )
    cost = src_norm[:, None] + tgt_norm[None, :] - 2.0 * cross
    return jnp.exp(-cost / epsilon_reg)


def local(src_cells, tgt_cells, src_mass, tgt_mass):
    src_block = lax.all_gather(src_cells, "tgt", axis=1, tiled=True)
    stored_tile = gibbs_tile(src_block, tgt_cells)

    def get_tile():
        return stored_tile

    col_scale = jnp.ones((tgt_cells.shape[1],), jnp.float32)
    row_scale = jnp.ones((src_block.shape[1],), jnp.float32)
    for sweep in range(ITERS):
        row_part = jnp.dot(get_tile(), col_scale, precision=lax.Precision.HIGHEST)
        row_total = lax.psum(row_part, "tgt")
        row_scale = src_mass / row_total
        col_part = jnp.dot(row_scale, get_tile(), precision=lax.Precision.HIGHEST)
        col_total = lax.psum(col_part, "src")
        col_scale = tgt_mass / col_total
    return (epsilon_reg * jnp.log(row_scale), epsilon_reg * jnp.log(col_scale))


def solution(mesh):
    placed = (P(None, ("src", "tgt")), P(None, "tgt"), P("src"), P("tgt"))
    return jax.shard_map(
        local, mesh=mesh, in_specs=placed, out_specs=(P("src"), P("tgt")), check_vma=False
    )
```

profile of v0, /device:TPU:1, one launch (start us, length us, event | category | flops | bytes accessed | tf_op | source)
XLA Modules:
  0.0 317.8 jit_solution(1861517863350990255)
XLA Ops:
  0.6 0.9 multiply_reduce_fusion.1
  1.6 34.9 %all_gather.3 = f32[50,4096]{1,0:T(8,128)S(1)} all-gather(f32[50,256]{1,0:T(8,128)} %param.4), channel_id=1, replica_groups=mesh['src'=32,'tgt'=16] {'tgt'}, dimensions={1}, use_global_device_ids=true | all-gather | bytes 870400 | tf_op jit(solution)/shard_map/all_gather | solution.py:21
  36.4 0.1 multiply_reduce_fusion
  36.5 9.2 %multiply_exponential_fusion = f32[4096,512]{1,0:T(8,128)S(1)} fusion(f32[50,4096]{1,0:T(8,128)S(1)} %all_gather.3, f32[50,512]{1,0:T(8,128)} %param.5, f32[512]{0:T(512)S(1)} %multiply_reduce_fusion.1, f32[4096]{0:T(1024)S(1)} %multiply_reduce_fusion), kind=kOutput, calls=%fused_computation | convolution fusion | flops 1268776960 | bytes 9328640 | tf_op jit(solution)/shard_map/dot_general | solution.py:13
  45.7 0.0 copy-start
  45.7 3.2 %copy-done = f32[4096,512]{1,0:T(8,128)} copy-done((f32[4096,512]{1,0:T(8,128)}, f32[4096,512]{1,0:T(8,128)S(1)}, u32[]{:S(2)}) %copy-start) | copy-done | bytes 8388632
  48.9 0.0 copy-start.1
  48.9 0.0 copy-start.2
  48.9 7.3 %fusion = f32[1,4096]{1,0:T(1,128)S(1)} fusion(f32[4096,512]{1,0:T(8,128)S(1)} %multiply_exponential_fusion), kind=kOutput, calls=%fused_computation.5 | convolution fusion | flops 25165824 | bytes 8404992 | tf_op jit(solution)/shard_map/dot_general | solution.py:30
  56.2 38.9 %psum.28 = f32[4096]{0:T(1024)S(1)} all-reduce(f32[4096]{0:T(1024)S(1)} %bitcast.18), channel_id=1, replica_groups=mesh['src'=32,'tgt'=16] {'tgt'}, use_global_device_ids=true, to_apply=%region_2.0 | all-reduce | flops 4096 | bytes 32768 | tf_op jit(solution)/shard_map/psum | solution.py:31
  95.1 0.0 copy-done.1
  95.1 6.4 %fusion.3 = f32[1,512]{1,0:T(1,128)S(1)} fusion(f32[4096,1]{0,1:T(1,128)S(1)} %bitcast.16, f32[4096,512]{1,0:T(8,128)} %copy-done), kind=kOutput, calls=%fused_computation.8 | convolution fusion | flops 25165824 | bytes 8407040 | tf_op jit(solution)/shard_map/dot_general | solution.py:33
  101.5 83.6 %psum.29 = f32[512]{0:T(512)S(1)} all-reduce(f32[512]{0:T(512)S(1)} %bitcast.22), channel_id=1, replica_groups=mesh['src'=32,'tgt'=16] {'src'}, use_global_device_ids=true, to_apply=%region_3.0 | all-reduce | flops 512 | bytes 4096 | tf_op jit(solution)/shard_map/psum | solution.py:34
  185.1 0.0 copy-done.2
  185.1 9.4 %fusion.4 = f32[1,4096]{1,0:T(1,128)S(1)} fusion(f32[4096,512]{1,0:T(8,128)} %copy-done, f32[512,1]{0,1:T(1,128)S(1)} %bitcast.20), kind=kOutput, calls=%fused_computation.9 | convolution fusion | flops 25165824 | bytes 8407040 | tf_op jit(solution)/shard_map/dot_general | solution.py:30
  194.6 39.5 %psum.30 = f32[4096]{0:T(1024)S(1)} all-reduce(f32[4096]{0:T(1024)S(1)} %bitcast.17), channel_id=1, replica_groups=mesh['src'=32,'tgt'=16] {'tgt'}, use_global_device_ids=true, to_apply=%region_4.0 | all-reduce | flops 4096 | bytes 32768 | tf_op jit(solution)/shard_map/psum | solution.py:31
  234.1 0.6 log_multiply_fusion
  234.7 6.4 %fusion.5 = f32[1,512]{1,0:T(1,128)S(1)} fusion(f32[4096,1]{0,1:T(1,128)S(1)} %bitcast.19, f32[4096,512]{1,0:T(8,128)} %copy-done), kind=kOutput, calls=%fused_computation.10 | convolution fusion | flops 25165824 | bytes 8407040 | tf_op jit(solution)/shard_map/dot_general | solution.py:33
  241.1 76.1 %psum.31 = f32[512]{0:T(512)S(1)} all-reduce(f32[512]{0:T(512)S(1)} %bitcast.21), channel_id=1, replica_groups=mesh['src'=32,'tgt'=16] {'src'}, use_global_device_ids=true, to_apply=%region_5.0 | all-reduce | flops 512 | bytes 4096 | tf_op jit(solution)/shard_map/psum | solution.py:34
  317.2 0.6 log_multiply_fusion.1
  (2 shorter events, 0.0 us)
Async XLA Ops:
  45.7 3.2 %copy-start = (f32[4096,512]{1,0:T(8,128)}, f32[4096,512]{1,0:T(8,128)S(1)}, u32[]{:S(2)}) copy-start(f32[4096,512]{1,0:T(8,128)S(1)} %multiply_exponential_fusion) | copy-start | bytes 25165828
  48.9 46.2 %copy-start.1 = (f32[4096]{0:T(1024)S(1)}, f32[4096]{0:T(1024)}, u32[]{:S(2)}) copy-start(f32[4096]{0:T(1024)} %param.6) | copy-start | bytes 49156
  48.9 136.2 %copy-start.2 = (f32[512]{0:T(512)S(1)}, f32[512]{0:T(512)}, u32[]{:S(2)}) copy-start(f32[512]{0:T(512)} %param.7) | copy-start | bytes 6148
where the time goes:
time: 318 us
  blocking collectives  273 us (86%)
  matrix products  38.6 us (12%)
  local copies, waits for them, and re-layouts  3.22 us (1%)
    psum x2, blocking collectives, local(): col_total = lax.psum(col_part, 'src')  160 us
    psum x2, blocking collectives, local(): row_total = lax.psum(row_part, 'tgt')  78.5 us
    all_gather x1, blocking collectives, local(): src_block = lax.all_gather(src_cells, 'tgt', axis=1, tiled=True)  34.9 us
    dot_general x2, matrix products, local(): row_part = jnp.dot(get_tile(), col_scale, precision=lax.Precision.HIGHEST)  16.7 us
    dot_general x2, matrix products, local(): col_part = jnp.dot(row_scale, get_tile(), precision=lax.Precision.HIGHEST)  12.7 us
    dot_general x1, matrix products, gibbs_tile(): jnp.dot(src_block.T, tgt_block, precision=lax.Precision.HIGHEST, preferre...  9.15 us

commit v1 on v0

--- a/solution.py
+++ b/solution.py
@@ -31,7 +31,10 @@
         row_total = lax.psum(row_part, "tgt")
         row_scale = src_mass / row_total
         col_part = jnp.dot(row_scale, get_tile(), precision=lax.Precision.HIGHEST)
-        col_total = lax.psum(col_part, "src")
+        peers, col_total = (lax.axis_size("src"), col_part)
+        for hop in [1 << k for k in range(peers.bit_length() - 1)]:
+            swap = [(i, i ^ hop) for i in range(peers)]
+            col_total = col_total + lax.ppermute(col_total, "src", swap)
         col_scale = tgt_mass / col_total
     return (epsilon_reg * jnp.log(row_scale), epsilon_reg * jnp.log(col_scale))
 

time: 318 us -> 246 us (0.77)
  blocking collectives: 273 us -> 113 us
  starting transfers between devices: 0 us -> 75.6 us
  waiting for transfers between devices: 0 us -> 10.6 us
    psum x2 -> x0, blocking collectives: 160 us -> none  [local(): col_total = lax.psum(col_part, 'src')]
    ppermute x0 -> x10, starting transfers between devices: none -> 75.6 us  [local(): col_total = col_total + lax.ppermute(col_total, 'src', swap)]
    ppermute x0 -> x10, waiting for transfers between devices: none -> 10.6 us  [local(): col_total = col_total + lax.ppermute(col_total, 'src', swap)]
  transfers between devices with their start and end apart: 0 -> 10, of which waited for: 0 -> 10; matrix products, arithmetic and copies ran while one was open for 0% -> 0% of each run, Pallas kernels for 0% -> 0%
where the time goes in v1:
time: 246 us; the launch traced here: 243 us
  blocking collectives  113 us (46%)
  starting transfers between devices  75.6 us (31%)
  matrix products  37.2 us (15%)
  waiting for transfers between devices  10.6 us (4%)
  local copies, waits for them, and re-layouts  3.22 us (1%)
    psum x2, blocking collectives, local(): row_total = lax.psum(row_part, 'tgt')  78.1 us
    ppermute x10, starting transfers between devices, local(): col_total = col_total + lax.ppermute(col_total, 'src', swap)  75.6 us
    all_gather x1, blocking collectives, local(): src_block = lax.all_gather(src_cells, 'tgt', axis=1, tiled=True)  34.9 us
    dot_general x2, matrix products, local(): row_part = jnp.dot(get_tile(), col_scale, precision=lax.Precision.HIGHEST)  14.5 us
    dot_general x2, matrix products, local(): col_part = jnp.dot(row_scale, get_tile(), precision=lax.Precision.HIGHEST)  13.6 us
    ppermute x10, waiting for transfers between devices, local(): col_total = col_total + lax.ppermute(col_total, 'src', swap)  10.6 us
    dot_general x1, matrix products, gibbs_tile(): jnp.dot(src_block.T, tgt_block, precision=lax.Precision.HIGHEST, preferre...  9.15 us
  transfers between devices with their start and end apart: 10, of which 10 were waited for; matrix products, arithmetic and copies ran while one was open for 0% of the time, Pallas kernels for 0%

profile of v1, /device:TPU:1, one launch (start us, length us, event | category | flops | bytes accessed | tf_op | source)
XLA Modules:
  0.0 242.6 jit_solution(16443424744875444006)
XLA Ops:
  1.6 34.9 %all_gather.3 = f32[50,4096]{1,0:T(8,128)S(1)} all-gather(f32[50,256]{1,0:T(8,128)} %param.4), channel_id=1, replica_groups=mesh['src'=32,'tgt'=16] {'tgt'}, dimensions={1}, use_global_device_ids=true | all-gather | bytes 870400 | tf_op jit(solution)/shard_map/all_gather | solution.py:21
  36.5 9.2 %multiply_exponential_fusion = f32[4096,512]{1,0:T(8,128)S(1)} fusion(f32[50,4096]{1,0:T(8,128)S(1)} %all_gather.3, f32[50,512]{1,0:T(8,128)} %param.5, f32[512]{0:T(512)S(1)} %multiply_reduce_fusion.1, f32[4096]{0:T(1024)S(1)} %multiply_reduce_fusion), kind=kOutput, calls=%fused_computation | convolution fusion | flops 1268776960 | bytes 9328640 | tf_op jit(solution)/shard_map/dot_general | solution.py:13
  45.7 3.2 %copy-done = f32[4096,512]{1,0:T(8,128)} copy-done((f32[4096,512]{1,0:T(8,128)}, f32[4096,512]{1,0:T(8,128)S(1)}, u32[]{:S(2)}) %copy-start) | copy-done | bytes 8388632
  48.9 7.3 %fusion = f32[1,4096]{1,0:T(1,128)S(1)} fusion(f32[4096,512]{1,0:T(8,128)S(1)} %multiply_exponential_fusion), kind=kOutput, calls=%fused_computation.7 | convolution fusion | flops 25165824 | bytes 8404992 | tf_op jit(solution)/shard_map/dot_general | solution.py:30
  56.2 38.9 %psum.14 = f32[4096]{0:T(1024)S(1)} all-reduce(f32[4096]{0:T(1024)S(1)} %bitcast.18), channel_id=1, replica_groups=mesh['src'=32,'tgt'=16] {'tgt'}, use_global_device_ids=true, to_apply=%region_2.0 | all-reduce | flops 4096 | bytes 32768 | tf_op jit(solution)/shard_map/psum | solution.py:31
  95.1 7.2 %fusion.3 = f32[1,512]{1,0:T(1,128)S(1)} fusion(f32[4096,1]{0,1:T(1,128)S(1)} %bitcast.16, f32[4096,512]{1,0:T(8,128)} %copy-done), kind=kOutput, calls=%fused_computation.10 | convolution fusion | flops 25165824 | bytes 8407040 | tf_op jit(solution)/shard_map/dot_general | solution.py:33
  102.3 23.2 %collective-permute-start = (f32[512]{0:T(512)S(1)}, f32[512]{0:T(512)S(1)}, u32[]{:S(2)}, u32[]{:S(2)}) collective-permute-start(f32[512]{0:T(512)S(1)} %bitcast.22), channel_id=1, source_target_pairs={{0,16},{16,0},{32,48},{48,32},{64,80},{80,64},{96,112},{112,96},{1... | collective-permute-start | bytes 6152 | tf_op jit(solution)/shard_map/ppermute | solution.py:37
  126.4 3.1 %collective-permute-start.1 = (f32[512]{0:T(512)S(1)}, f32[512]{0:T(512)S(1)}, u32[]{:S(2)}, u32[]{:S(2)}) collective-permute-start(f32[512]{0:T(512)S(1)} %add.50), channel_id=1, source_target_pairs={{0,32},{16,48},{32,0},{48,16},{64,96},{80,112},{96,64},{112,80},{1... | collective-permute-start | bytes 6152 | tf_op jit(solution)/shard_map/ppermute | solution.py:37
  129.5 1.2 collective-permute-done.1
  130.7 4.6 %collective-permute-start.2 = (f32[512]{0:T(512)S(1)}, f32[512]{0:T(512)S(1)}, u32[]{:S(2)}, u32[]{:S(2)}) collective-permute-start(f32[512]{0:T(512)S(1)} %add.51), channel_id=1, source_target_pairs={{0,64},{16,80},{32,96},{48,112},{64,0},{80,16},{96,32},{112,48},{1... | collective-permute-start | bytes 6152 | tf_op jit(solution)/shard_map/ppermute | solution.py:37
  135.4 1.2 collective-permute-done.2
  136.5 3.2 %collective-permute-start.3 = (f32[512]{0:T(512)S(1)}, f32[512]{0:T(512)S(1)}, u32[]{:S(2)}, u32[]{:S(2)}) collective-permute-start(f32[512]{0:T(512)S(1)} %add.52), channel_id=1, source_target_pairs={{0,128},{16,144},{32,160},{48,176},{64,192},{80,208},{96,224},{112... | collective-permute-start | bytes 6152 | tf_op jit(solution)/shard_map/ppermute | solution.py:37
  139.7 1.1 collective-permute-done.3
  140.9 4.8 %collective-permute-start.4 = (f32[512]{0:T(512)S(1)}, f32[512]{0:T(512)S(1)}, u32[]{:S(2)}, u32[]{:S(2)}) collective-permute-start(f32[512]{0:T(512)S(1)} %add.53), channel_id=1, source_target_pairs={{0,256},{16,272},{32,288},{48,304},{64,320},{80,336},{96,352},{112... | collective-permute-start | bytes 6152 | tf_op jit(solution)/shard_map/ppermute | solution.py:37
  146.7 7.2 %fusion.4 = f32[1,4096]{1,0:T(1,128)S(1)} fusion(f32[4096,512]{1,0:T(8,128)S(1)} %copy-done.1, f32[512,1]{0,1:T(1,128)S(1)} %bitcast.24), kind=kOutput, calls=%fused_computation.11 | convolution fusion | flops 25165824 | bytes 8407040 | tf_op jit(solution)/shard_map/dot_general | solution.py:30
  153.9 39.2 %psum.15 = f32[4096]{0:T(1024)S(1)} all-reduce(f32[4096]{0:T(1024)S(1)} %bitcast.17), channel_id=1, replica_groups=mesh['src'=32,'tgt'=16] {'tgt'}, use_global_device_ids=true, to_apply=%region_3.0 | all-reduce | flops 4096 | bytes 32768 | tf_op jit(solution)/shard_map/psum | solution.py:31
  193.7 6.4 %fusion.5 = f32[1,512]{1,0:T(1,128)S(1)} fusion(f32[4096,1]{0,1:T(1,128)S(1)} %bitcast.19, f32[4096,512]{1,0:T(8,128)} %copy-done), kind=kOutput, calls=%fused_computation.12 | convolution fusion | flops 25165824 | bytes 8407040 | tf_op jit(solution)/shard_map/dot_general | solution.py:33
  200.1 20.9 %collective-permute-start.5 = (f32[512]{0:T(512)S(1)}, f32[512]{0:T(512)S(1)}, u32[]{:S(2)}, u32[]{:S(2)}) collective-permute-start(f32[512]{0:T(512)S(1)} %bitcast.20), channel_id=1, source_target_pairs={{0,16},{16,0},{32,48},{48,32},{64,80},{80,64},{96,112},{112,96},{1... | collective-permute-start | bytes 6152 | tf_op jit(solution)/shard_map/ppermute | solution.py:37
  221.7 3.1 %collective-permute-start.6 = (f32[512]{0:T(512)S(1)}, f32[512]{0:T(512)S(1)}, u32[]{:S(2)}, u32[]{:S(2)}) collective-permute-start(f32[512]{0:T(512)S(1)} %add.55), channel_id=1, source_target_pairs={{0,32},{16,48},{32,0},{48,16},{64,96},{80,112},{96,64},{112,80},{1... | collective-permute-start | bytes 6152 | tf_op jit(solution)/shard_map/ppermute | solution.py:37
  224.8 1.2 collective-permute-done.6
  226.0 4.6 %collective-permute-start.7 = (f32[512]{0:T(512)S(1)}, f32[512]{0:T(512)S(1)}, u32[]{:S(2)}, u32[]{:S(2)}) collective-permute-start(f32[512]{0:T(512)S(1)} %add.56), channel_id=1, source_target_pairs={{0,64},{16,80},{32,96},{48,112},{64,0},{80,16},{96,32},{112,48},{1... | collective-permute-start | bytes 6152 | tf_op jit(solution)/shard_map/ppermute | solution.py:37
  230.7 1.2 collective-permute-done.7
  231.9 3.2 %collective-permute-start.8 = (f32[512]{0:T(512)S(1)}, f32[512]{0:T(512)S(1)}, u32[]{:S(2)}, u32[]{:S(2)}) collective-permute-start(f32[512]{0:T(512)S(1)} %add.57), channel_id=1, source_target_pairs={{0,128},{16,144},{32,160},{48,176},{64,192},{80,208},{96,224},{112... | collective-permute-start | bytes 6152 | tf_op jit(solution)/shard_map/ppermute | solution.py:37
  236.2 4.8 %collective-permute-start.9 = (f32[512]{0:T(512)S(1)}, f32[512]{0:T(512)S(1)}, u32[]{:S(2)}, u32[]{:S(2)}) collective-permute-start(f32[512]{0:T(512)S(1)} %add.58), channel_id=1, source_target_pairs={{0,256},{16,272},{32,288},{48,304},{64,320},{80,336},{96,352},{112... | collective-permute-start | bytes 6152 | tf_op jit(solution)/shard_map/ppermute | solution.py:37
  (26 shorter events, 7.0 us)
Async XLA Ops:
  45.7 3.2 %copy-start = (f32[4096,512]{1,0:T(8,128)}, f32[4096,512]{1,0:T(8,128)S(1)}, u32[]{:S(2)}) copy-start(f32[4096,512]{1,0:T(8,128)S(1)} %multiply_exponential_fusion) | copy-start | bytes 25165828
  48.9 46.2 %copy-start.2 = (f32[4096]{0:T(1024)S(1)}, f32[4096]{0:T(1024)}, u32[]{:S(2)}) copy-start(f32[4096]{0:T(1024)} %param.6) | copy-start | bytes 49156
  48.9 97.8 %copy-start.3 = (f32[512]{0:T(512)S(1)}, f32[512]{0:T(512)}, u32[]{:S(2)}) copy-start(f32[512]{0:T(512)} %param.7) | copy-start | bytes 6148
  95.1 51.6 %copy-start.1 = (f32[4096,512]{1,0:T(8,128)S(1)}, f32[4096,512]{1,0:T(8,128)}, u32[]{:S(2)}) copy-start(f32[4096,512]{1,0:T(8,128)} %copy-done) | copy-start | bytes 25165828
  102.3 24.0 %collective-permute-start = (f32[512]{0:T(512)S(1)}, f32[512]{0:T(512)S(1)}, u32[]{:S(2)}, u32[]{:S(2)}) collective-permute-start(f32[512]{0:T(512)S(1)} %bitcast.22), channel_id=1, source_target_pairs={{0,16},{16,0},{32,48},{48,32},{64,80},{80,64},{96,112},{112,96},{1... | collective-permute-start | bytes 6152 | tf_op jit(solution)/shard_map/ppermute | solution.py:37
  126.4 4.3 %collective-permute-start.1 = (f32[512]{0:T(512)S(1)}, f32[512]{0:T(512)S(1)}, u32[]{:S(2)}, u32[]{:S(2)}) collective-permute-start(f32[512]{0:T(512)S(1)} %add.50), channel_id=1, source_target_pairs={{0,32},{16,48},{32,0},{48,16},{64,96},{80,112},{96,64},{112,80},{1... | collective-permute-start | bytes 6152 | tf_op jit(solution)/shard_map/ppermute | solution.py:37
  130.7 5.8 %collective-permute-start.2 = (f32[512]{0:T(512)S(1)}, f32[512]{0:T(512)S(1)}, u32[]{:S(2)}, u32[]{:S(2)}) collective-permute-start(f32[512]{0:T(512)S(1)} %add.51), channel_id=1, source_target_pairs={{0,64},{16,80},{32,96},{48,112},{64,0},{80,16},{96,32},{112,48},{1... | collective-permute-start | bytes 6152 | tf_op jit(solution)/shard_map/ppermute | solution.py:37
  136.5 4.3 %collective-permute-start.3 = (f32[512]{0:T(512)S(1)}, f32[512]{0:T(512)S(1)}, u32[]{:S(2)}, u32[]{:S(2)}) collective-permute-start(f32[512]{0:T(512)S(1)} %add.52), channel_id=1, source_target_pairs={{0,128},{16,144},{32,160},{48,176},{64,192},{80,208},{96,224},{112... | collective-permute-start | bytes 6152 | tf_op jit(solution)/shard_map/ppermute | solution.py:37
  140.9 5.8 %collective-permute-start.4 = (f32[512]{0:T(512)S(1)}, f32[512]{0:T(512)S(1)}, u32[]{:S(2)}, u32[]{:S(2)}) collective-permute-start(f32[512]{0:T(512)S(1)} %add.53), channel_id=1, source_target_pairs={{0,256},{16,272},{32,288},{48,304},{64,320},{80,336},{96,352},{112... | collective-permute-start | bytes 6152 | tf_op jit(solution)/shard_map/ppermute | solution.py:37
  200.1 21.7 %collective-permute-start.5 = (f32[512]{0:T(512)S(1)}, f32[512]{0:T(512)S(1)}, u32[]{:S(2)}, u32[]{:S(2)}) collective-permute-start(f32[512]{0:T(512)S(1)} %bitcast.20), channel_id=1, source_target_pairs={{0,16},{16,0},{32,48},{48,32},{64,80},{80,64},{96,112},{112,96},{1... | collective-permute-start | bytes 6152 | tf_op jit(solution)/shard_map/ppermute | solution.py:37
  221.7 4.3 %collective-permute-start.6 = (f32[512]{0:T(512)S(1)}, f32[512]{0:T(512)S(1)}, u32[]{:S(2)}, u32[]{:S(2)}) collective-permute-start(f32[512]{0:T(512)S(1)} %add.55), channel_id=1, source_target_pairs={{0,32},{16,48},{32,0},{48,16},{64,96},{80,112},{96,64},{112,80},{1... | collective-permute-start | bytes 6152 | tf_op jit(solution)/shard_map/ppermute | solution.py:37
  226.0 5.8 %collective-permute-start.7 = (f32[512]{0:T(512)S(1)}, f32[512]{0:T(512)S(1)}, u32[]{:S(2)}, u32[]{:S(2)}) collective-permute-start(f32[512]{0:T(512)S(1)} %add.56), channel_id=1, source_target_pairs={{0,64},{16,80},{32,96},{48,112},{64,0},{80,16},{96,32},{112,48},{1... | collective-permute-start | bytes 6152 | tf_op jit(solution)/shard_map/ppermute | solution.py:37
  231.9 4.3 %collective-permute-start.8 = (f32[512]{0:T(512)S(1)}, f32[512]{0:T(512)S(1)}, u32[]{:S(2)}, u32[]{:S(2)}) collective-permute-start(f32[512]{0:T(512)S(1)} %add.57), channel_id=1, source_target_pairs={{0,128},{16,144},{32,160},{48,176},{64,192},{80,208},{96,224},{112... | collective-permute-start | bytes 6152 | tf_op jit(solution)/shard_map/ppermute | solution.py:37
  236.2 5.8 %collective-permute-start.9 = (f32[512]{0:T(512)S(1)}, f32[512]{0:T(512)S(1)}, u32[]{:S(2)}, u32[]{:S(2)}) collective-permute-start(f32[512]{0:T(512)S(1)} %add.58), channel_id=1, source_target_pairs={{0,256},{16,272},{32,288},{48,304},{64,320},{80,336},{96,352},{112... | collective-permute-start | bytes 6152 | tf_op jit(solution)/shard_map/ppermute | solution.py:37
